TPU v7x, 128 devices: a whole 4x4x4 slice. The times are simulated.
128 devices in a mesh: replica: 4 (over z), shard: 16 (over y, x_lo, core), tensor: 2 (over x_hi).
Axes of the slice: x: 4 (x_hi: 2, x_lo: 2; x = x_hi * 2 + x_lo), y: 4, z: 4, core: 2. Of those that a mesh axis runs over, the one named last changes fastest.
Arguments:
- trained_up: bfloat16 [4, 1024, 4096], P('replica', None, 'tensor'), may hold values from -6 to 6
- trained_down: bfloat16 [4, 4096, 1024], P('replica', 'tensor'), may hold values from -6 to 6
- trained_embed: bfloat16 [4, 32768, 1024], P('replica', ('shard', 'tensor')), may hold values from -6 to 6
- trained_norm: bfloat16 [4, 2, 1024], P('replica'), may hold values from 0.099609375 to 1.8984375
- master_up: float32 [1024, 4096], P(('replica', 'shard', 'tensor')), may hold values from -6 to 6
- moment_up: float32 [1024, 4096], P(('replica', 'shard', 'tensor')), may hold values from -4 to 4
- master_down: float32 [2, 2048, 1024], P('tensor', ('replica', 'shard')), may hold values from -6 to 6
- moment_down: float32 [2, 2048, 1024], P('tensor', ('replica', 'shard')), may hold values from -4 to 4
- master_embed: float32 [32, 1024, 1024], P(('shard', 'tensor'), 'replica'), may hold values from -6 to 6
- moment_embed: float32 [32, 1024, 64], P(('shard', 'tensor'), 'replica'), may hold values from -4 to 4
- master_norm: float32 [2, 1024], replicated, may hold values from 0.1 to 1.9
- moment_norm: float32 [2, 1024], replicated, may hold values from -2 to 2
- embed_basis: float32 [1024, 64], replicated, may hold values from -0.1875 to 0.1875
Outputs:
- recast_up: bfloat16 [1024, 4096], P(None, 'tensor')
- recast_down: bfloat16 [4096, 1024], P('tensor')
- recast_embed: bfloat16 [32768, 1024], P(('shard', 'tensor'))
- recast_norm: bfloat16 [2, 1024], replicated
- stored_up: float32 [1024, 4096], P(('replica', 'shard', 'tensor'))
- velocity_up: float32 [1024, 4096], P(('replica', 'shard', 'tensor'))
- stored_down: float32 [2, 2048, 1024], P('tensor', ('replica', 'shard'))
- velocity_down: float32 [2, 2048, 1024], P('tensor', ('replica', 'shard'))
- stored_embed: float32 [32, 1024, 1024], P(('shard', 'tensor'), 'replica')
- velocity_embed: float32 [32, 1024, 64], P(('shard', 'tensor'), 'replica')
- stored_norm: float32 [2, 1024], replicated
- velocity_norm: float32 [2, 1024], replicated
All inputs are finite; a program needn't handle non-finite values.
Results may differ from a plain program's by a relative error of at most 0.012.
Values may be sent and summed in bfloat16 or wider, within the bound.
A program may use at most 128 MiB of HBM per device.

v0:
```python
import jax
import jax.numpy as jnp
from jax import lax
from jax.sharding import PartitionSpec as P


def outer_step(master, moment, summed, groups):
    difference = master - summed / groups
    velocity = 0.5 * moment + difference
    return (master - 0.7 * (difference + 0.5 * velocity), velocity)


def body(
    trained_up,
    trained_down,
    trained_embed,
    trained_norm,
    master_up,
    moment_up,
    master_down,
    moment_down,
    master_embed,
    moment_embed,
    master_norm,
    moment_norm,
    embed_basis,
):
    replicas = lax.axis_size("replica")
    shards = lax.axis_size("shard")
    tensors = lax.axis_size("tensor")
    shard_pos = lax.axis_index("shard")
    width = embed_basis.shape[0]
    rows_up = master_up.shape[0]
    half_cols = trained_up.shape[2]
    rows_down = master_down.shape[1]
    up_blocks = trained_up[0].reshape(replicas, shards, tensors, rows_up, half_cols)
    up_own = lax.dynamic_index_in_dim(up_blocks, shard_pos, 1, keepdims=False)
    down_blocks = trained_down[0].reshape(replicas, shards, rows_down, width)
    down_own = lax.dynamic_index_in_dim(down_blocks, shard_pos, 1, keepdims=False)
    up_summed, down_summed = (
        lax.psum_scatter(
            up_own.astype(jnp.float32).astype(jnp.bfloat16),
            "replica",
            scatter_dimension=0,
            tiled=True,
        ).astype(jnp.float32),
        lax.psum_scatter(
            down_own.astype(jnp.float32).astype(jnp.bfloat16),
            "replica",
            scatter_dimension=0,
            tiled=True,
        ).astype(jnp.float32),
    )
    up_summed = lax.all_to_all(up_summed, "tensor", split_axis=1, concat_axis=3, tiled=True)
    stored_up, velocity_up = outer_step(
        master_up, moment_up, up_summed.reshape(rows_up, half_cols * tensors), replicas
    )
    stored_down, velocity_down = outer_step(master_down, moment_down, down_summed, replicas)
    norm_summed = lax.psum(trained_norm[0].astype(jnp.float32), "replica")
    stored_norm, velocity_norm = outer_step(master_norm, moment_norm, norm_summed, replicas)
    embed_own = master_embed[0]
    rows_embed = embed_own.shape[0]
    embed_terms = trained_embed[0].reshape(replicas, rows_embed, width).astype(jnp.float32)
    embed_summed = lax.psum_scatter(
        embed_terms.astype(jnp.bfloat16), "replica", scatter_dimension=0, tiled=True
    ).astype(jnp.float32)[0]
    coefficient = jnp.dot(
        embed_own - embed_summed / replicas, embed_basis, precision=lax.Precision.HIGHEST
    )
    velocity_rows = 0.5 * moment_embed[0] + coefficient
    stored_rows = embed_own - 0.7 * jnp.dot(
        coefficient + 0.5 * velocity_rows, embed_basis.T, precision=lax.Precision.HIGHEST
    )
    up_piece = lax.all_to_all(
        stored_up.astype(jnp.bfloat16), "tensor", split_axis=1, concat_axis=0, tiled=True
    )
    down_piece = stored_down[0].astype(jnp.bfloat16)
    recast_up, recast_down = (
        lax.all_gather(up_piece, ("replica", "shard"), axis=0, tiled=True),
        lax.all_gather(down_piece, ("replica", "shard"), axis=0, tiled=True),
    )
    recast_embed = lax.all_gather(stored_rows.astype(jnp.bfloat16), "replica", axis=0, tiled=True)
    return (
        recast_up,
        recast_down,
        recast_embed,
        stored_norm.astype(jnp.bfloat16),
        stored_up,
        velocity_up,
        stored_down,
        velocity_down,
        stored_rows[None],
        velocity_rows[None],
        stored_norm,
        velocity_norm,
    )


def solution(mesh):
    in_specs = (
        P("replica", None, "tensor"),
        P("replica", "tensor", None),
        P("replica", ("shard", "tensor"), None),
        P("replica", None, None),
        P(("replica", "shard", "tensor"), None),
        P(("replica", "shard", "tensor"), None),
        P("tensor", ("replica", "shard"), None),
        P("tensor", ("replica", "shard"), None),
        P(("shard", "tensor"), "replica", None),
        P(("shard", "tensor"), "replica", None),
        P(),
        P(),
        P(),
    )
    out_specs = (
        P(None, "tensor"),
        P("tensor", None),
        P(("shard", "tensor"), None),
        P(),
        P(("replica", "shard", "tensor"), None),
        P(("replica", "shard", "tensor"), None),
        P("tensor", ("replica", "shard"), None),
        P("tensor", ("replica", "shard"), None),
        P(("shard", "tensor"), "replica", None),
        P(("shard", "tensor"), "replica", None),
        P(),
        P(),
    )
    return jax.shard_map(body, mesh=mesh, in_specs=in_specs, out_specs=out_specs, check_vma=False)
```

profile of v0, /device:TPU:1, one launch (start us, length us, event | category | flops | bytes accessed | tf_op | source)
XLA Modules:
  0.0 376.6 jit_solution(8853071086595991756)
XLA Ops:
  7.2 0.0 copy-start
  7.2 0.0 copy-start.1
  7.2 0.0 copy-start.4
  7.2 0.0 reduce-scatter.6.cloned.1.call-start
  7.3 0.0 copy-start.12
  7.3 0.7 reduce-scatter.6.cloned.1.call-update
  7.9 0.0 copy-start.7
  8.0 0.0 copy-start.8
  8.0 0.0 all-reduce.3.cloned.1.call-start
  8.0 1.7 copy_bitcast_fusion
  9.7 0.0 all-reduce.3.cloned.1.call-update
  9.7 0.0 reduce-scatter.4.cloned.1.call-start
  9.8 0.0 copy-start.11
  9.8 1.7 dynamic-slice_bitcast_fusion
  11.5 0.0 reduce-scatter.4.cloned.1.call-update
  11.5 0.0 all-gather.7.cloned.1.call-start
  11.6 32.1 %reduce-scatter.6.cloned.1.call-done = bf16[1,256,1024]{2,1,0:T(8,128)(2,1)} async-done(((bf16[4,256,1024]{2,1,0:T(8,128)(2,1)}), bf16[1,256,1024]{2,1,0:T(8,128)(2,1)}) %reduce-scatter.6.cloned.1.call-update) | async-done | bytes 524304 | tf_op jit(solution)/shard_map/reduce_scatter | solution.py:64
  43.6 0.0 copy-done
  43.6 0.0 copy-done.1
  43.6 2.2 fusion.1
  45.8 0.0 copy-done.4
  45.8 2.2 fusion.16
  48.0 0.0 all-gather.7.cloned.1.call-update
  48.1 0.0 all-gather.5.cloned.1.call-start
  48.1 0.0 copy-done.12
  48.1 0.6 dynamic-slice
  48.7 37.3 %all-reduce.3.cloned.1.call-done = bf16[4,2,8,2048]{3,2,0,1:T(8,128)(2,1)} async-done(((bf16[4,2,8,2048]{3,2,0,1:T(8,128)(2,1)}), bf16[4,2,8,2048]{3,2,0,1:T(8,128)(2,1)}) %all-reduce.3.cloned.1.call-update) | async-done | bytes 262160
  86.0 1.5 dynamic-slice_convert_fusion
  87.5 8.6 %all_to_all.28 = f32[1,2,8,2048]{3,2,0,1:T(8,128)S(1)} all-to-all(f32[1,2,8,2048]{3,2,0,1:T(8,128)S(1)} %dynamic-slice_convert_fusion), channel_id=1, replica_groups=mesh['replica'=4,'shard'=16,'tensor'=2] {'tensor'}, dimensions={1} | all-to-all | bytes 262144 | tf_op jit(solution)/shard_map/all_to_all | solution.py:54
  96.1 0.7 fusion.15
  96.9 7.5 %all_to_all.29 = bf16[8,2,2048]{2,0,1:T(8,128)(2,1)} all-to-all(bf16[8,2,2048]{2,0,1:T(8,128)(2,1)S(1)} %bitcast.53), channel_id=1, replica_groups=mesh['replica'=4,'shard'=16,'tensor'=2] {'tensor'}, dimensions={1} | all-to-all | bytes 131072 | tf_op jit(solution)/shard_map/all_to_all | solution.py:74
  104.4 0.0 all-gather.5.cloned.1.call-update
  104.4 0.0 all-gather.9.cloned.1.call-start
  104.4 5.8 %reduce-scatter.4.cloned.1.call-done = bf16[1,32,1024]{2,1,0:T(8,128)(2,1)} async-done(((bf16[4,32,1024]{2,1,0:T(8,128)(2,1)}), bf16[1,32,1024]{2,1,0:T(8,128)(2,1)}) %reduce-scatter.4.cloned.1.call-update) | async-done | bytes 65552 | tf_op jit(solution)/shard_map/reduce_scatter | solution.py:47
  110.3 0.0 copy-done.6
  110.3 1.6 fusion.14
  111.9 0.0 all-gather.9.cloned.1.call-update
  111.9 6.9 %psum.7 = f32[2,1024]{1,0:T(2,128)S(1)} all-reduce(f32[2,1024]{1,0:T(2,128)S(1)} %bitcast_convert_fusion), channel_id=1, replica_groups=mesh['replica'=4,'shard'=16,'tensor'=2] {'replica'}, use_global_device_ids=true, to_apply=%region_3.4 | all-reduce | flops 2048 | bytes 16384 | tf_op jit(solution)/shard_map/psum | solution.py:59
  118.9 0.6 fusion.13
  119.5 0.6 fusion.8
  120.2 25.0 %all-gather.7.cloned.1.call-done = bf16[1024,1024]{1,0:T(8,128)(2,1)} async-done(((bf16[256,1024]{1,0:T(8,128)(2,1)}), bf16[1024,1024]{1,0:T(8,128)(2,1)}) %all-gather.7.cloned.1.call-update) | async-done | bytes 2097168 | tf_op jit(solution)/shard_map/all_gather | solution.py:82
  145.2 108.0 %all-gather.5.cloned.1.call-done = bf16[1024,2048]{1,0:T(8,128)(2,1)} async-done(((bf16[16,2048]{1,0:T(8,128)(2,1)}), bf16[1024,2048]{1,0:T(8,128)(2,1)}) %all-gather.5.cloned.1.call-update) | async-done | bytes 4194320 | tf_op jit(solution)/shard_map/all_gather | solution.py:79
  253.2 107.3 %all-gather.9.cloned.1.call-done = bf16[1,2048,1024]{2,1,0:T(8,128)(2,1)} async-done(((bf16[1,32,1024]{2,1,0:T(8,128)(2,1)}), bf16[1,2048,1024]{2,1,0:T(8,128)(2,1)}) %all-gather.9.cloned.1.call-update) | async-done | bytes 4194320 | tf_op jit(solution)/shard_map/all_gather | solution.py:80
  360.4 4.9 %copy.39 = bf16[1024,2048]{1,0:T(8,128)(2,1)} copy(bf16[1024,2048]{1,0:T(8,128)(2,1)} %all-gather.5.cloned.1.call-done) | data formatting | bytes 8388608
  365.4 0.0 copy-done.2
  365.4 2.1 copy.40
  367.5 1.0 copy-done.3
  368.5 1.3 copy.41
  (14 shorter events, 0.0 us)
Async XLA Ops:
  7.2 36.5 %copy-start = (f32[1024,64]{0,1:T(8,128)S(1)}, f32[1024,64]{0,1:T(8,128)}, u32[]{:S(2)}) copy-start(f32[1024,64]{0,1:T(8,128)} %param.25) | copy-start | bytes 786436
  7.2 36.5 %copy-start.1 = (f32[1,256,1024]{2,1,0:T(8,128)S(1)}, f32[1,256,1024]{2,1,0:T(8,128)}, u32[]{:S(2)}) copy-start(f32[1,256,1024]{2,1,0:T(8,128)} %param.21) | copy-start | bytes 3145732
  7.2 38.6 %copy-start.4 = (f32[1,256,64]{1,2,0:T(8,128)S(1)}, f32[1,256,64]{1,2,0:T(8,128)}, u32[]{:S(2)}) copy-start(f32[1,256,64]{1,2,0:T(8,128)} %param.22) | copy-start | bytes 196612
  7.2 36.4 %reduce-scatter.6.cloned.1.call-start = ((), (), s32[]{:S(2)}) async-start(), calls=%async_computation.6 | async-start | bytes 2621440 | tf_op jit(solution)/shard_map/reduce_scatter | solution.py:64
  7.3 40.9 %copy-start.12 = (u32[128]{0:T(128)S(1)}, u32[128]{0:T(128)}, u32[]{:S(2)}) copy-start(u32[128]{0:T(128)} %constant.47) | copy-start | bytes 1540
  7.9 88.2 %copy-start.7 = (f32[8,4096]{1,0:T(8,128)S(1)}, f32[8,4096]{1,0:T(8,128)}, u32[]{:S(2)}) copy-start(f32[8,4096]{1,0:T(8,128)} %param.17) | copy-start | bytes 393220
  8.0 88.2 %copy-start.8 = (f32[8,4096]{1,0:T(8,128)S(1)}, f32[8,4096]{1,0:T(8,128)}, u32[]{:S(2)}) copy-start(f32[8,4096]{1,0:T(8,128)} %param.18) | copy-start | bytes 393220
  8.0 78.0 %all-reduce.3.cloned.1.call-start = ((), (), s32[]{:S(2)}) async-start(), calls=%async_computation.9 | async-start | bytes 524288
  9.7 100.6 %copy-start.5 = (f32[1,32,1024]{2,1,0:T(8,128)S(1)}, f32[1,32,1024]{2,1,0:T(8,128)}, u32[]{:S(2)}) copy-start(f32[1,32,1024]{2,1,0:T(8,128)} %param.19) | copy-start | bytes 393220
  9.7 100.6 %copy-start.6 = (f32[1,32,1024]{2,1,0:T(8,128)S(1)}, f32[1,32,1024]{2,1,0:T(8,128)}, u32[]{:S(2)}) copy-start(f32[1,32,1024]{2,1,0:T(8,128)} %param.20) | copy-start | bytes 393220
  9.7 100.6 %reduce-scatter.4.cloned.1.call-start = ((), (), s32[]{:S(2)}) async-start(), calls=%async_computation.5 | async-start | bytes 327680 | tf_op jit(solution)/shard_map/reduce_scatter | solution.py:47
  9.8 102.1 %copy-start.11 = (bf16[1,2,1024]{2,1,0:T(2,128)(2,1)S(1)}, bf16[1,2,1024]{2,1,0:T(2,128)(2,1)}, u32[]{:S(2)}) copy-start(bf16[1,2,1024]{2,1,0:T(2,128)(2,1)} %param.16) | copy-start | bytes 12292
  11.5 107.4 %copy-start.9 = (f32[2,1024]{1,0:T(2,128)S(1)}, f32[2,1024]{1,0:T(2,128)}, u32[]{:S(2)}) copy-start(f32[2,1024]{1,0:T(2,128)} %param.23) | copy-start | bytes 24580
  11.5 107.4 %copy-start.10 = (f32[2,1024]{1,0:T(2,128)S(1)}, f32[2,1024]{1,0:T(2,128)}, u32[]{:S(2)}) copy-start(f32[2,1024]{1,0:T(2,128)} %param.24) | copy-start | bytes 24580
  11.5 133.6 %all-gather.7.cloned.1.call-start = ((), (), s32[]{:S(2)}) async-start(), calls=%async_computation.7 | async-start | bytes 2621440 | tf_op jit(solution)/shard_map/all_gather | solution.py:82
  48.1 205.1 %all-gather.5.cloned.1.call-start = ((), (), s32[]{:S(2)}) async-start(), calls=%async_computation.4 | async-start | bytes 4259840 | tf_op jit(solution)/shard_map/all_gather | solution.py:79
  104.4 256.0 %all-gather.9.cloned.1.call-start = ((), (), s32[]{:S(2)}) async-start(), calls=%async_computation.8 | async-start | bytes 4259840 | tf_op jit(solution)/shard_map/all_gather | solution.py:80
  360.4 4.9 %copy-start.2 = (bf16[1,2048,1024]{2,1,0:T(8,128)(2,1)S(1)}, bf16[1,2048,1024]{2,1,0:T(8,128)(2,1)}, u32[]{:S(2)}) copy-start(bf16[1,2048,1024]{2,1,0:T(8,128)(2,1)} %all-gather.9.cloned.1.call-done) | copy-start | bytes 12582916
  365.4 3.1 copy-start.3
Sparse Core Ops, SparseCore 0:
  10.4 33.1 reduce-scatter.5
  46.7 39.3 all-reduce.2
  89.0 21.2 reduce-scatter.3
  112.5 32.6 all-gather.6
  146.9 106.2 all-gather.4
  255.4 104.9 all-gather.8
where the time goes:
time: 377 us
  waiting for transfers between devices  316 us (84%)
  blocking collectives  23 us (6%)
  between operations  14.3 us (4%)
  local copies, waits for them, and re-layouts  13.4 us (4%)
  other arithmetic  5.09 us (1%)
  matrix products  4.38 us (1%)
    all_gather x1, waiting for transfers between devices, body(): lax.all_gather(up_piece, ('replica', 'shard'), axis=0, tiled=True)  108 us
    all_gather x1, waiting for transfers between devices, body(): lax.all_gather(down_piece, ('replica', 'shard'), axis=0, tiled=True)  107 us
    unnamed x7, waiting for transfers between devices  38.1 us
    reduce_scatter x1, waiting for transfers between devices, body(): lax.psum_scatter(embed_terms.astype(jnp.bfloat16), 'replica', scatter_dim...  32.1 us
    all_gather x1, waiting for transfers between devices, body(): lax.all_gather(stored_rows.astype(jnp.bfloat16), 'replica', axis=0, tiled...  25 us
    unnamed x30, local copies, waits for them, and re-layouts  10 us
    all_to_all x1, blocking collectives, body(): lax.all_to_all(up_summed, 'tensor', split_axis=1, concat_axis=3, tiled=True)  8.59 us
  transfers between devices with their start and end apart: 6, of which 6 were waited for; matrix products, arithmetic and copies ran while one was open for 4% of the time, Pallas kernels for 0%

commit v1 on v0

--- a/solution.py
+++ b/solution.py
@@ -1,7 +1,19 @@
+import functools
 import jax
 import jax.numpy as jnp
 from jax import lax
 from jax.sharding import PartitionSpec as P
+
+
+def fields_answer(xin, shard_axis, k_dim):
+    w2 = jnp.concatenate(tuple((xin for _ in range(lax.axis_size(shard_axis)))), axis=k_dim)
+    part_now = lax.all_to_all(
+        w2, axis_name=shard_axis, split_axis=k_dim, concat_axis=k_dim, tiled=True
+    )
+    return part_now
+
+
+scan_face = functools.partial(fields_answer, shard_axis="replica", k_dim=0)
 
 
 def outer_step(master, moment, summed, groups):
@@ -79,7 +91,7 @@
         lax.all_gather(up_piece, ("replica", "shard"), axis=0, tiled=True),
         lax.all_gather(down_piece, ("replica", "shard"), axis=0, tiled=True),
     )
-    recast_embed = lax.all_gather(stored_rows.astype(jnp.bfloat16), "replica", axis=0, tiled=True)
+    recast_embed = scan_face(stored_rows.astype(jnp.bfloat16))
     return (
         recast_up,
         recast_down,

time: 377 us -> 353 us (0.936)
  waiting for transfers between devices: 316 us -> 261 us
  blocking collectives: 23 us -> 50.1 us
    all_gather x1, waiting for transfers between devices: 108 us -> 73.4 us  [body(): lax.all_gather(up_piece, ('replica', 'shard'), axis=0, tiled=True)]
    psum x1, blocking collectives: 6.93 us -> 34 us  [body(): norm_summed = lax.psum(trained_norm[0].astype(jnp.float32), 'replica')]
    all_gather x1 -> x0, waiting for transfers between devices: 25 us -> none  [body(): lax.all_gather(stored_rows.astype(jnp.bfloat16), 'replica', axis=0, tiled...]
    unnamed x7 -> x6, waiting for transfers between devices: 38.1 us -> 41.8 us
    unnamed x30 -> x26, local copies, waits for them, and re-layouts: 10 us -> 9.57 us
  transfers between devices with their start and end apart: 6 -> 6, of which waited for: 6 -> 5; matrix products, arithmetic and copies ran while one was open for 4% -> 4% of each run, Pallas kernels for 0% -> 0%
where the time goes in v1:
time: 353 us
  waiting for transfers between devices  261 us (74%)
  blocking collectives  50.1 us (14%)
  between operations  14 us (4%)
  local copies, waits for them, and re-layouts  13.1 us (4%)
  other arithmetic  6.69 us (2%)
  matrix products  4.21 us (1%)
  starting transfers between devices  3.81 us (1%)
    all_gather x1, waiting for transfers between devices, body(): lax.all_gather(down_piece, ('replica', 'shard'), axis=0, tiled=True)  107 us
    all_gather x1, waiting for transfers between devices, body(): lax.all_gather(up_piece, ('replica', 'shard'), axis=0, tiled=True)  73.4 us
    unnamed x6, waiting for transfers between devices  41.8 us
    psum x1, blocking collectives, body(): norm_summed = lax.psum(trained_norm[0].astype(jnp.float32), 'replica')  34 us
    reduce_scatter x1, waiting for transfers between devices, body(): lax.psum_scatter(embed_terms.astype(jnp.bfloat16), 'replica', scatter_dim...  32.4 us
    unnamed x26, local copies, waits for them, and re-layouts  9.57 us
    all_to_all x1, blocking collectives, body(): lax.all_to_all(up_summed, 'tensor', split_axis=1, concat_axis=3, tiled=True)  8.59 us
    all_to_all x1, blocking collectives, body(): lax.all_to_all(stored_up.astype(jnp.bfloat16), 'tensor', split_axis=1, co...  7.5 us
  transfers between devices with their start and end apart: 6, of which 5 were waited for; matrix products, arithmetic and copies ran while one was open for 4% of the time, Pallas kernels for 0%

profile of v1, /device:TPU:1, one launch (start us, length us, event | category | flops | bytes accessed | tf_op | source)
XLA Modules:
  0.0 352.7 jit_solution(13000381479985502903)
XLA Ops:
  7.2 0.0 copy-start
  7.2 0.0 copy-start.6
  7.2 0.0 copy-start.7
  7.2 0.0 copy-start.4
  7.2 0.0 copy-start.5
  7.2 0.0 copy-start.1
  7.2 0.0 copy-start.3
  7.3 0.0 all-reduce.3.cloned.1.call-start
  7.3 1.8 copy_bitcast_fusion
  9.1 0.0 all-reduce.3.cloned.1.call-update
  9.2 0.0 reduce-scatter.4.cloned.1.call-start
  9.2 1.7 dynamic-slice_bitcast_fusion
  10.9 0.0 reduce-scatter.4.cloned.1.call-update
  10.9 0.0 reduce-scatter.6.cloned.1.call-start
  11.0 0.7 reduce-scatter.6.cloned.1.call-update
  11.6 0.0 all-gather.4.cloned.1.call-start
  11.7 1.2 dynamic-slice
  12.9 41.1 %all-reduce.3.cloned.1.call-done = bf16[4,2,8,2048]{3,2,0,1:T(8,128)(2,1)} async-done(((bf16[4,2,8,2048]{3,2,0,1:T(8,128)(2,1)}), bf16[4,2,8,2048]{3,2,0,1:T(8,128)(2,1)}) %all-reduce.3.cloned.1.call-update) | async-done | bytes 262160
  54.0 1.5 dynamic-slice_convert_fusion
  55.5 8.6 %all_to_all.40 = f32[1,2,8,2048]{3,2,0,1:T(8,128)S(1)} all-to-all(f32[1,2,8,2048]{3,2,0,1:T(8,128)S(1)} %dynamic-slice_convert_fusion), channel_id=1, replica_groups=mesh['replica'=4,'shard'=16,'tensor'=2] {'tensor'}, dimensions={1} | all-to-all | bytes 262144 | tf_op jit(solution)/shard_map/all_to_all | solution.py:66
  64.1 0.0 copy-done.6
  64.1 0.0 copy-done.7
  64.2 0.7 fusion.15
  64.9 7.5 %all_to_all.41 = bf16[8,2,2048]{2,0,1:T(8,128)(2,1)} all-to-all(bf16[8,2,2048]{2,0,1:T(8,128)(2,1)S(1)} %bitcast.56), channel_id=1, replica_groups=mesh['replica'=4,'shard'=16,'tensor'=2] {'tensor'}, dimensions={1} | all-to-all | bytes 131072 | tf_op jit(solution)/shard_map/all_to_all | solution.py:86
  72.4 0.0 all-gather.4.cloned.1.call-update
  72.4 0.0 all-gather.6.cloned.1.call-start
  72.5 6.0 %reduce-scatter.4.cloned.1.call-done = bf16[1,32,1024]{2,1,0:T(8,128)(2,1)} async-done(((bf16[4,32,1024]{2,1,0:T(8,128)(2,1)}), bf16[1,32,1024]{2,1,0:T(8,128)(2,1)}) %reduce-scatter.4.cloned.1.call-update) | async-done | bytes 65552 | tf_op jit(solution)/shard_map/reduce_scatter | solution.py:59
  78.4 0.0 copy-done.4
  78.4 0.0 copy-done.5
  78.4 1.6 fusion.14
  80.0 0.0 all-gather.6.cloned.1.call-update
  80.1 32.4 %reduce-scatter.6.cloned.1.call-done = bf16[1,256,1024]{2,1,0:T(8,128)(2,1)} async-done(((bf16[4,256,1024]{2,1,0:T(8,128)(2,1)}), bf16[1,256,1024]{2,1,0:T(8,128)(2,1)}) %reduce-scatter.6.cloned.1.call-update) | async-done | bytes 524304 | tf_op jit(solution)/shard_map/reduce_scatter | solution.py:76
  112.4 0.0 copy-done.1
  112.4 2.2 fusion.1
  114.6 0.0 copy-start.8
  114.6 0.0 copy-start.9
  114.6 2.0 fusion.16
  116.7 1.6 pad_maximum_fusion
  118.3 3.6 %all-to-all-start.2 = ((bf16[4,256,1024]{2,1,0:T(8,128)(2,1)}), bf16[4,256,1024]{2,1,0:T(8,128)(2,1)S(1)}, u32[]{:S(2)}, u32[]{:S(2)}) async-start(bf16[4,256,1024]{2,1,0:T(8,128)(2,1)} %bitcast.15), calls=%async_computation.4 | async-start | bytes 4194304 | tf_op jit(solution)/shard_map/all_to_all | solution.py:10
  121.9 34.0 %psum.7 = f32[2,1024]{1,0:T(2,128)S(1)} all-reduce(f32[2,1024]{1,0:T(2,128)S(1)} %bitcast_convert_fusion), channel_id=1, replica_groups=mesh['replica'=4,'shard'=16,'tensor'=2] {'replica'}, use_global_device_ids=true, to_apply=%region_3.4 | all-reduce | flops 2048 | bytes 16384 | tf_op jit(solution)/shard_map/psum | solution.py:71
  155.9 0.6 fusion.13
  156.5 0.6 fusion.8
  157.2 0.0 all-to-all-done.2
  157.2 73.4 %all-gather.4.cloned.1.call-done = bf16[1024,2048]{1,0:T(8,128)(2,1)} async-done(((bf16[16,2048]{1,0:T(8,128)(2,1)}), bf16[1024,2048]{1,0:T(8,128)(2,1)}) %all-gather.4.cloned.1.call-update) | async-done | bytes 4194320 | tf_op jit(solution)/shard_map/all_gather | solution.py:91
  230.6 107.4 %all-gather.6.cloned.1.call-done = bf16[1,2048,1024]{2,1,0:T(8,128)(2,1)} async-done(((bf16[1,32,1024]{2,1,0:T(8,128)(2,1)}), bf16[1,2048,1024]{2,1,0:T(8,128)(2,1)}) %all-gather.6.cloned.1.call-update) | async-done | bytes 4194320 | tf_op jit(solution)/shard_map/all_gather | solution.py:92
  337.9 4.9 %copy.39 = bf16[1024,2048]{1,0:T(8,128)(2,1)} copy(bf16[1024,2048]{1,0:T(8,128)(2,1)} %all-gather.4.cloned.1.call-done) | data formatting | bytes 8388608
  342.9 2.0 copy.40
  344.9 1.3 copy.41
  (10 shorter events, 0.0 us)
Async XLA Ops:
  7.2 105.3 %copy-start = (f32[1024,64]{0,1:T(8,128)S(1)}, f32[1024,64]{0,1:T(8,128)}, u32[]{:S(2)}) copy-start(f32[1024,64]{0,1:T(8,128)} %param.25) | copy-start | bytes 786436
  7.2 56.9 %copy-start.6 = (f32[8,4096]{1,0:T(8,128)S(1)}, f32[8,4096]{1,0:T(8,128)}, u32[]{:S(2)}) copy-start(f32[8,4096]{1,0:T(8,128)} %param.17) | copy-start | bytes 393220
  7.2 56.9 %copy-start.7 = (f32[8,4096]{1,0:T(8,128)S(1)}, f32[8,4096]{1,0:T(8,128)}, u32[]{:S(2)}) copy-start(f32[8,4096]{1,0:T(8,128)} %param.18) | copy-start | bytes 393220
  7.2 71.2 %copy-start.4 = (f32[1,32,1024]{2,1,0:T(8,128)S(1)}, f32[1,32,1024]{2,1,0:T(8,128)}, u32[]{:S(2)}) copy-start(f32[1,32,1024]{2,1,0:T(8,128)} %param.19) | copy-start | bytes 393220
  7.2 71.2 %copy-start.5 = (f32[1,32,1024]{2,1,0:T(8,128)S(1)}, f32[1,32,1024]{2,1,0:T(8,128)}, u32[]{:S(2)}) copy-start(f32[1,32,1024]{2,1,0:T(8,128)} %param.20) | copy-start | bytes 393220
  7.2 105.2 %copy-start.1 = (f32[1,256,1024]{2,1,0:T(8,128)S(1)}, f32[1,256,1024]{2,1,0:T(8,128)}, u32[]{:S(2)}) copy-start(f32[1,256,1024]{2,1,0:T(8,128)} %param.21) | copy-start | bytes 3145732
  7.2 107.4 %copy-start.3 = (f32[1,256,64]{1,2,0:T(8,128)S(1)}, f32[1,256,64]{1,2,0:T(8,128)}, u32[]{:S(2)}) copy-start(f32[1,256,64]{1,2,0:T(8,128)} %param.22) | copy-start | bytes 196612
  7.3 46.8 %all-reduce.3.cloned.1.call-start = ((), (), s32[]{:S(2)}) async-start(), calls=%async_computation.9 | async-start | bytes 524288
  9.2 69.3 %reduce-scatter.4.cloned.1.call-start = ((), (), s32[]{:S(2)}) async-start(), calls=%async_computation.6 | async-start | bytes 327680 | tf_op jit(solution)/shard_map/reduce_scatter | solution.py:59
  10.9 101.5 %reduce-scatter.6.cloned.1.call-start = ((), (), s32[]{:S(2)}) async-start(), calls=%async_computation.7 | async-start | bytes 2621440 | tf_op jit(solution)/shard_map/reduce_scatter | solution.py:76
  11.6 218.9 %all-gather.4.cloned.1.call-start = ((), (), s32[]{:S(2)}) async-start(), calls=%async_computation.5 | async-start | bytes 4259840 | tf_op jit(solution)/shard_map/all_gather | solution.py:91
  72.4 265.5 %all-gather.6.cloned.1.call-start = ((), (), s32[]{:S(2)}) async-start(), calls=%async_computation.8 | async-start | bytes 4259840 | tf_op jit(solution)/shard_map/all_gather | solution.py:92
  114.6 41.3 %copy-start.8 = (f32[2,1024]{1,0:T(2,128)S(1)}, f32[2,1024]{1,0:T(2,128)}, u32[]{:S(2)}) copy-start(f32[2,1024]{1,0:T(2,128)} %param.23) | copy-start | bytes 24580
  114.6 41.3 %copy-start.9 = (f32[2,1024]{1,0:T(2,128)S(1)}, f32[2,1024]{1,0:T(2,128)}, u32[]{:S(2)}) copy-start(f32[2,1024]{1,0:T(2,128)} %param.24) | copy-start | bytes 24580
  116.7 5.2 %copy-start.10 = (bf16[1,2,1024]{2,1,0:T(2,128)(2,1)S(1)}, bf16[1,2,1024]{2,1,0:T(2,128)(2,1)}, u32[]{:S(2)}) copy-start(bf16[1,2,1024]{2,1,0:T(2,128)(2,1)} %param.16) | copy-start | bytes 12292
  118.3 38.9 %all-to-all-start.2 = ((bf16[4,256,1024]{2,1,0:T(8,128)(2,1)}), bf16[4,256,1024]{2,1,0:T(8,128)(2,1)S(1)}, u32[]{:S(2)}, u32[]{:S(2)}) async-start(bf16[4,256,1024]{2,1,0:T(8,128)(2,1)} %bitcast.15), calls=%async_computation.4 | async-start | bytes 4194304 | tf_op jit(solution)/shard_map/all_to_all | solution.py:10
  337.9 4.9 %copy-start.2 = (bf16[1,2048,1024]{2,1,0:T(8,128)(2,1)S(1)}, bf16[1,2048,1024]{2,1,0:T(8,128)(2,1)}, u32[]{:S(2)}) copy-start(bf16[1,2048,1024]{2,1,0:T(8,128)(2,1)} %all-gather.6.cloned.1.call-done) | copy-start | bytes 12582916
Sparse Core Ops, SparseCore 0:
  11.0 42.9 all-reduce.2
  57.1 21.2 reduce-scatter.3
  80.8 31.5 reduce-scatter.5
  114.1 116.3 all-gather.3
  232.8 105.0 all-gather.5
